TPU v7x, 32 devices: a whole 2x2x4 slice. The times are simulated.
32 devices in a mesh: wide: 16 (over z, y, x), clus: 2 (over core).
Axes of the slice: x: 2, y: 2, z: 4, core: 2. Of those that a mesh axis runs over, the one named last changes fastest.
Arguments:
- duals: bfloat16 [96, 64, 3840], P(None, ('wide', 'clus')), may hold values from -6 to 6
- kernel: bfloat16 [64, 6, 3840], P(('wide', 'clus')), may hold values from -0.29882812 to 0.29882812
- sub_counts: int32 [32], P(('wide', 'clus')), may hold values from 1 to 2, as said below
- dual_sizes: int32 [64], P(('wide', 'clus')), may hold values from 1920 to 3840, as said below
- cluster_factor: float32 [16, 24, 24], P('wide'), as said below
- coarse_map: int32 [16, 24], P('wide'), may hold values from 0 to 383, as said below
- coarse_inverse: float32 [384, 384], P(None, 'clus'), as said below
Outputs:
- projected: bfloat16 [96, 64, 3840], P(None, ('wide', 'clus'))
Inputs may be any that keep to these rules, and one draw needn't show every extreme that they name: `sub_counts`: each device holds 1 to 2 subdomains; some device holds 2. `dual_sizes`: some slot has the full 3840. `coarse_map`: the rows of cluster w map into the 48 global rows that begin at w * 24, counted modulo 384. `cluster_factor`: lower triangular with diagonal entries between 1 and 2. `coarse_inverse`: diagonal entries between 1 and 2.
All inputs are finite; a program needn't handle non-finite values.
Results may differ from a plain program's by a relative error of at most 0.0018.
Values sent between devices are 32-bit elements; how exact they have to be, the bound alone decides.
No kernel may reach another device: no remote copies, remote signals or barrier semaphores. Data moves between devices by JAX's collectives and lax.ppermute only.
A program may use at most 64 MiB of HBM per device.

v0:
```python
import jax
import jax.numpy as jnp
from jax import lax
from jax.sharding import PartitionSpec as P


def per_device(duals, kernel, sub_counts, dual_sizes, cluster_factor, coarse_map, coarse_inverse):
    rhs_count, sub_count, dual_width = duals.shape
    mode_count = kernel.shape[1]
    hi = lax.Precision.HIGHEST
    position = lax.broadcasted_iota(jnp.int32, (sub_count, dual_width), 1)
    slot_index = lax.broadcasted_iota(jnp.int32, (sub_count, dual_width), 0)
    active = (position < dual_sizes[:, None]) & (slot_index < sub_counts[0])
    masked = jnp.where(active[:, None, :], kernel, jnp.zeros_like(kernel))
    local = jnp.einsum("rsi,ski->rsk", duals, masked, preferred_element_type=jnp.float32)
    local = local.reshape(rhs_count, sub_count * mode_count)
    cluster_vec = lax.all_gather(local, "clus", axis=1, tiled=True)
    lower = cluster_factor[0]
    rows_map = coarse_map[0]
    cluster_rows = rows_map.shape[0]
    global_rows = coarse_inverse.shape[0]
    forward = lax.linalg.triangular_solve(lower, cluster_vec.T, left_side=True, lower=True).T
    one_hot = (
        rows_map[:, None] == lax.broadcasted_iota(jnp.int32, (cluster_rows, global_rows), 1)
    ).astype(jnp.float32)
    part_sum = jnp.dot(forward, one_hot, precision=hi)
    gsum = lax.psum(part_sum, "wide")
    beta_part = jnp.dot(gsum, coarse_inverse, precision=hi)
    beta = lax.all_gather(beta_part, "clus", axis=1, tiled=True)
    back = jnp.dot(beta, one_hot.T, precision=hi)
    corr = lax.linalg.triangular_solve(
        lower, (forward - back).T, left_side=True, lower=True, transpose_a=True
    )
    own_rows = lax.dynamic_slice_in_dim(
        corr, lax.axis_index("clus") * sub_count * mode_count, sub_count * mode_count, 0
    )
    own_corr = own_rows.T.reshape(rhs_count, sub_count, mode_count).astype(jnp.bfloat16)
    delta = jnp.einsum("rsk,ski->rsi", own_corr, masked, preferred_element_type=jnp.float32)
    return (duals.astype(jnp.float32) - delta).astype(jnp.bfloat16)


def solution(mesh):
    in_specs = (
        P(None, ("wide", "clus"), None),
        P(("wide", "clus"), None, None),
        P(("wide", "clus")),
        P(("wide", "clus")),
        P("wide", None, None),
        P("wide", None),
        P(None, "clus"),
    )
    out_specs = P(None, ("wide", "clus"), None)
    return jax.shard_map(
        per_device, mesh=mesh, in_specs=in_specs, out_specs=out_specs, check_vma=False
    )
```

profile of v0, /device:TPU:0, one launch (start us, length us, event | category | flops | bytes accessed | tf_op | source)
XLA Modules:
  0.0 140.0 jit_solution(6165059862386261918)
XLA Ops:
  6.5 0.0 copy-start
  6.5 0.0 copy-start.2
  6.5 0.0 all-reduce.2.cloned.1.call-start
  7.3 0.7 fusion.16
  8.0 1.8 %custom-call.5 = f32[1,24,24]{1,2,0:T(8,128)S(1)} custom-call(f32[1,24,24]{2,1,0:T(8,128)S(1)} %fusion.16), custom_call_target="InvertDiagBlocksLowerTriangular" | custom-call | tf_op jit(solution)/shard_map/triangular_solve | solution.py:31
  9.8 0.8 compare_and_fusion
  10.6 1.0 broadcast_select_fusion
  11.6 0.0 copy-start.1
  11.6 2.0 %fusion.4 = f32[96,2,6]{0,2,1:T(8,128)S(1)} fusion(bf16[96,2,3840]{2,1,0:T(2,128)(2,1)} %param.7, bf16[2,6,3840]{2,0,1:T(2,128)(2,1)S(1)} %broadcast_select_fusion), kind=kOutput, calls=%fused_computation.6 | convolution fusion | flops 8847360 | bytes 1571328 | tf_op jit(solution)/shard_map/rsi,ski->rsk/dot_general | solution.py:15
  13.5 2.0 %all-gather = f32[2,12,96]{2,1,0:T(8,128)S(1)} all-gather(f32[1,12,96]{2,1,0:T(8,128)S(1)} %bitcast.34), channel_id=1, replica_groups=mesh['wide'=16,'clus'=2] {'clus'}, dimensions={0}, use_global_device_ids=true | all-gather | bytes 13824 | tf_op jit(solution)/shard_map/all_gather | solution.py:17
  15.5 0.2 fusion.14
  15.7 0.0 copy-done.2
  15.7 0.9 fusion.9
  16.7 0.0 all-reduce.2.cloned.1.call-update
  16.7 109.5 %all-reduce.2.cloned.1.call-done = f32[96,384]{1,0:T(8,128)} async-done(((f32[96,384]{1,0:T(8,128)}), f32[96,384]{1,0:T(8,128)}) %all-reduce.2.cloned.1.call-update) | async-done | bytes 147472 | tf_op jit(solution)/shard_map/psum | solution.py:27
  126.2 0.0 copy-done
  126.2 1.3 fusion.18
  127.5 1.9 %all_gather.7 = f32[96,384]{0,1:T(8,128)S(1)} all-gather(f32[96,192]{0,1:T(8,128)S(1)} %fusion.18), channel_id=1, replica_groups=mesh['wide'=16,'clus'=2] {'clus'}, dimensions={1}, use_global_device_ids=true | all-gather | bytes 221184 | tf_op jit(solution)/shard_map/all_gather | solution.py:29
  129.5 0.2 convolution_subtract_fusion
  129.7 0.1 fusion.12
  129.9 0.0 copy-done.1
  129.9 0.6 fusion.1
  130.5 2.6 %copy.23 = bf16[96,2,3840]{2,1,0:T(2,128)(2,1)} copy(bf16[96,2,3840]{2,0,1:T(8,128)(2,1)S(1)} %fusion.1) | data formatting | bytes 2949120 | tf_op jit(solution)/shard_map/convert_element_type | solution.py:39
  (5 shorter events, 0.1 us)
Async XLA Ops:
  6.5 119.7 %copy-start = (f32[384,192]{0,1:T(8,128)S(1)}, f32[384,192]{0,1:T(8,128)}, u32[]{:S(2)}) copy-start(f32[384,192]{0,1:T(8,128)} %param.13) | copy-start | bytes 884740
  6.5 9.2 %copy-start.2 = (s32[1,24]{1,0:T(1,128)S(1)}, s32[1,24]{1,0:T(1,128)}, u32[]{:S(2)}) copy-start(s32[1,24]{1,0:T(1,128)} %param.12) | copy-start | bytes 292
  6.5 119.7 %all-reduce.2.cloned.1.call-start = ((), (), s32[]{:S(2)}) async-start(), calls=%async_computation | async-start | bytes 294912 | tf_op jit(solution)/shard_map/psum | solution.py:27
  11.6 118.3 %copy-start.1 = (bf16[96,2,3840]{2,1,0:T(2,128)(2,1)S(1)}, bf16[96,2,3840]{2,1,0:T(2,128)(2,1)}, u32[]{:S(2)}) copy-start(bf16[96,2,3840]{2,1,0:T(2,128)(2,1)} %param.7) | copy-start | bytes 4423684
Sparse Core Ops, SparseCore 0:
  16.8 109.3 all-reduce.1
where the time goes:
time: 140 us
  waiting for transfers between devices  110 us (79%)
  between operations  14.2 us (10%)
  matrix products  5.34 us (4%)
  other arithmetic  4.31 us (3%)
  blocking collectives  3.92 us (3%)
  local copies, waits for them, and re-layouts  2.7 us (2%)
    psum x1, waiting for transfers between devices, per_device(): gsum = lax.psum(part_sum, 'wide')  110 us
  transfers between devices with their start and end apart: 1, of which 1 were waited for; matrix products, arithmetic and copies ran while one was open for 0% of the time, Pallas kernels for 0%

commit v1 on v0

--- a/solution.py
+++ b/solution.py
@@ -2,6 +2,15 @@
 import jax.numpy as jnp
 from jax import lax
 from jax.sharding import PartitionSpec as P
+
+
+def add_in_pairs(array, axis):
+    n_dev = lax.axis_size(axis)
+    total, hop = (array, 1)
+    while hop < n_dev:
+        total = total + lax.ppermute(total, axis, [(i, i ^ hop) for i in range(n_dev)])
+        hop = 2 * hop
+    return total
 
 
 def per_device(duals, kernel, sub_counts, dual_sizes, cluster_factor, coarse_map, coarse_inverse):
@@ -24,7 +33,7 @@
         rows_map[:, None] == lax.broadcasted_iota(jnp.int32, (cluster_rows, global_rows), 1)
     ).astype(jnp.float32)
     part_sum = jnp.dot(forward, one_hot, precision=hi)
-    gsum = lax.psum(part_sum, "wide")
+    gsum = add_in_pairs(part_sum, "wide")
     beta_part = jnp.dot(gsum, coarse_inverse, precision=hi)
     beta = lax.all_gather(beta_part, "clus", axis=1, tiled=True)
     back = jnp.dot(beta, one_hot.T, precision=hi)

time: 140 us -> 41.3 us (0.29)
  waiting for transfers between devices: 110 us -> 16 us
  between operations: 14.2 us -> 0.8 us
  starting transfers between devices: 0.01 us -> 9.54 us
  matrix products: 5.34 us -> 3.67 us
    psum x1 -> x0, waiting for transfers between devices: 110 us -> none  [per_device(): gsum = lax.psum(part_sum, 'wide')]
    ppermute x0 -> x4, waiting for transfers between devices: none -> 16 us  [add_in_pairs(): lax.ppermute(total, axis, [(i, i ^ hop) for i in range(n_dev)])]
    ppermute x0 -> x4, starting transfers between devices: none -> 9.54 us  [add_in_pairs(): lax.ppermute(total, axis, [(i, i ^ hop) for i in range(n_dev)])]
  transfers between devices with their start and end apart: 1 -> 4, of which waited for: 1 -> 4; matrix products, arithmetic and copies ran while one was open for 0% -> 0% of each run, Pallas kernels for 0% -> 0%
where the time goes in v1:
time: 41.3 us; the launch traced here: 41.1 us
  waiting for transfers between devices  16 us (39%)
  starting transfers between devices  9.54 us (23%)
  other arithmetic  4.35 us (11%)
  blocking collectives  4.05 us (10%)
  matrix products  3.67 us (9%)
  local copies, waits for them, and re-layouts  2.69 us (7%)
  between operations  0.8 us (2%)
    ppermute x4, waiting for transfers between devices, add_in_pairs(): lax.ppermute(total, axis, [(i, i ^ hop) for i in range(n_dev)])  16 us
    ppermute x4, starting transfers between devices, add_in_pairs(): lax.ppermute(total, axis, [(i, i ^ hop) for i in range(n_dev)])  9.54 us
    convert_element_type x1, local copies, waits for them, and re-layouts, per_device(): return (duals.astype(jnp.float32) - delta).astype(jnp.bfloat16)  2.63 us
    another operation x2, other arithmetic, per_device(): lax.linalg.triangular_solve(lower, (forward - back).T, left_side=True, lo...  2.55 us
    all_gather x1, blocking collectives, per_device(): cluster_vec = lax.all_gather(local, 'clus', axis=1, tiled=True)  2.1 us
    all_gather x1, blocking collectives, per_device(): beta = lax.all_gather(beta_part, 'clus', axis=1, tiled=True)  1.95 us
    dot_general x1, matrix products, per_device(): jnp.einsum('rsi,ski->rsk', duals, masked, preferred_element_type=jnp.floa...  1.85 us
    select_n x1, other arithmetic, per_device(): masked = jnp.where(active[:, None, :], kernel, jnp.zeros_like(kernel))  0.98 us
  transfers between devices with their start and end apart: 4, of which 4 were waited for; matrix products, arithmetic and copies ran while one was open for 0% of the time, Pallas kernels for 0%

profile of v1, /device:TPU:0, one launch (start us, length us, event | category | flops | bytes accessed | tf_op | source)
XLA Modules:
  0.0 41.1 jit_solution(3064429446144641165)
XLA Ops:
  0.0 0.0 copy-start
  0.0 0.0 copy-start.2
  0.7 0.7 %fusion.18 = f32[1,24,24]{2,1,0:T(8,128)S(1)} fusion(f32[1,24,24]{2,1,0:T(8,128)} %param.11), kind=kLoop, calls=%fused_computation.22 | loop fusion | flops 1152 | bytes 4608 | tf_op jit(solution)/shard_map/triangular_solve | solution.py:40
  1.4 1.8 %custom-call.5 = f32[1,24,24]{1,2,0:T(8,128)S(1)} custom-call(f32[1,24,24]{2,1,0:T(8,128)S(1)} %fusion.18), custom_call_target="InvertDiagBlocksLowerTriangular" | custom-call | tf_op jit(solution)/shard_map/triangular_solve | solution.py:40
  3.3 0.8 %compare_and_fusion = pred[2,3840]{1,0:T(4,128)(4,1)S(1)} fusion(pred[2]{0:T(512)(128)(4,1)S(1)} %iota_compare_fusion.4, s32[2]{0:T(128)} %param.10), kind=kLoop, calls=%fused_computation.12 | loop fusion | flops 15360 | bytes 7690 | tf_op jit(solution)/shard_map/and | solution.py:22
  4.0 1.0 %broadcast_select_fusion = bf16[2,6,3840]{2,0,1:T(2,128)(2,1)S(1)} fusion(bf16[2,6,3840]{2,0,1:T(2,128)(2,1)} %param.8, pred[2,3840]{1,0:T(4,128)(4,1)S(1)} %compare_and_fusion), kind=kLoop, calls=%fused_computation.7 | loop fusion | flops 46080 | bytes 192000 | tf_op jit(solution)/shard_map/jit(_where)/select_n | solution.py:23
  5.0 1.9 %fusion.4 = f32[96,2,6]{0,2,1:T(8,128)S(1)} fusion(bf16[96,2,3840]{2,1,0:T(2,128)(2,1)} %param.7, bf16[2,6,3840]{2,0,1:T(2,128)(2,1)S(1)} %broadcast_select_fusion), kind=kOutput, calls=%fused_computation.6 | convolution fusion | flops 8847360 | bytes 1571328 | tf_op jit(solution)/shard_map/rsi,ski->rsk/dot_general | solution.py:24
  6.9 0.0 copy-start.1
  6.9 2.1 %all-gather = f32[2,12,96]{2,1,0:T(8,128)S(1)} all-gather(f32[1,12,96]{2,1,0:T(8,128)S(1)} %bitcast.33), channel_id=1, replica_groups=mesh['wide'=16,'clus'=2] {'clus'}, dimensions={0}, use_global_device_ids=true | all-gather | bytes 13824 | tf_op jit(solution)/shard_map/all_gather | solution.py:26
  9.0 0.2 fusion.16
  9.2 0.0 copy-done.2
  9.2 0.3 fusion.11
  9.5 2.9 %collective-permute-start = (f32[96,384]{1,0:T(8,128)S(1)}, f32[96,384]{1,0:T(8,128)S(1)}, u32[]{:S(2)}, u32[]{:S(2)}) collective-permute-start(f32[96,384]{1,0:T(8,128)S(1)} %fusion.11), channel_id=1, source_target_pairs={{0,2},{2,0},{4,6},{6,4},{8,10},{10,8},{12,14},{14,12},{16,18},{18,... | collective-permute-start | bytes 442376 | tf_op jit(solution)/shard_map/ppermute | solution.py:11
  12.4 4.2 %collective-permute-done = f32[96,384]{1,0:T(8,128)S(1)} collective-permute-done((f32[96,384]{1,0:T(8,128)S(1)}, f32[96,384]{1,0:T(8,128)S(1)}, u32[]{:S(2)}, u32[]{:S(2)}) %collective-permute-start) | collective-permute-done | bytes 147488 | tf_op jit(solution)/shard_map/ppermute | solution.py:11
  16.6 1.8 %collective-permute-start.1 = (f32[96,384]{1,0:T(8,128)S(1)}, f32[96,384]{1,0:T(8,128)S(1)}, u32[]{:S(2)}, u32[]{:S(2)}) collective-permute-start(f32[96,384]{1,0:T(8,128)S(1)} %add.19), channel_id=1, source_target_pairs={{0,4},{2,6},{4,0},{6,2},{8,12},{10,14},{12,8},{14,10},{16,20},{18,... | collective-permute-start | bytes 442376 | tf_op jit(solution)/shard_map/ppermute | solution.py:11
  18.4 3.6 %collective-permute-done.1 = f32[96,384]{1,0:T(8,128)S(1)} collective-permute-done((f32[96,384]{1,0:T(8,128)S(1)}, f32[96,384]{1,0:T(8,128)S(1)}, u32[]{:S(2)}, u32[]{:S(2)}) %collective-permute-start.1) | collective-permute-done | bytes 147488 | tf_op jit(solution)/shard_map/ppermute | solution.py:11
  22.0 1.7 %collective-permute-start.2 = (f32[96,384]{1,0:T(8,128)S(1)}, f32[96,384]{1,0:T(8,128)S(1)}, u32[]{:S(2)}, u32[]{:S(2)}) collective-permute-start(f32[96,384]{1,0:T(8,128)S(1)} %add.20), channel_id=1, source_target_pairs={{0,8},{2,10},{4,12},{6,14},{8,0},{10,2},{12,4},{14,6},{16,24},{18,... | collective-permute-start | bytes 442376 | tf_op jit(solution)/shard_map/ppermute | solution.py:11
  23.7 3.5 %collective-permute-done.2 = f32[96,384]{1,0:T(8,128)S(1)} collective-permute-done((f32[96,384]{1,0:T(8,128)S(1)}, f32[96,384]{1,0:T(8,128)S(1)}, u32[]{:S(2)}, u32[]{:S(2)}) %collective-permute-start.2) | collective-permute-done | bytes 147488 | tf_op jit(solution)/shard_map/ppermute | solution.py:11
  27.2 3.1 %collective-permute-start.3 = (f32[96,384]{1,0:T(8,128)S(1)}, f32[96,384]{1,0:T(8,128)S(1)}, u32[]{:S(2)}, u32[]{:S(2)}) collective-permute-start(f32[96,384]{1,0:T(8,128)S(1)} %add.21), channel_id=1, source_target_pairs={{0,16},{2,18},{4,20},{6,22},{8,24},{10,26},{12,28},{14,30},{16,0},... | collective-permute-start | bytes 442376 | tf_op jit(solution)/shard_map/ppermute | solution.py:11
  30.4 4.7 %collective-permute-done.3 = f32[96,384]{1,0:T(8,128)S(1)} collective-permute-done((f32[96,384]{1,0:T(8,128)S(1)}, f32[96,384]{1,0:T(8,128)S(1)}, u32[]{:S(2)}, u32[]{:S(2)}) %collective-permute-start.3) | collective-permute-done | bytes 147488 | tf_op jit(solution)/shard_map/ppermute | solution.py:11
  35.1 0.0 copy-done
  35.1 0.4 %fusion.7 = f32[96,192]{0,1:T(8,128)S(1)} fusion(f32[384,192]{0,1:T(8,128)S(1)} %copy-done, f32[96,384]{1,0:T(8,128)S(1)} %add.21, f32[96,384]{1,0:T(8,128)S(1)} %collective-permute-done.3), kind=kOutput, calls=%fused_computation.8 | convolution fusion | flops 84971520 | bytes 663552 | tf_op jit(solution)/shard_map/dot_general | solution.py:37
  35.5 1.9 %all_gather.7 = f32[96,384]{0,1:T(8,128)S(1)} all-gather(f32[96,192]{0,1:T(8,128)S(1)} %fusion.7), channel_id=1, replica_groups=mesh['wide'=16,'clus'=2] {'clus'}, dimensions={1}, use_global_device_ids=true | all-gather | bytes 221184 | tf_op jit(solution)/shard_map/all_gather | solution.py:38
  37.4 0.2 convolution_subtract_fusion
  37.7 0.1 fusion.14
  37.8 0.0 copy-done.1
  37.9 0.6 %fusion.1 = bf16[96,2,3840]{2,0,1:T(8,128)(2,1)S(1)} fusion(bf16[96,2,6]{0,2,1:T(8,128)(2,1)S(1)} %convert_element_type.19, bf16[96,2,3840]{2,1,0:T(2,128)(2,1)S(1)} %copy-done.1, bf16[2,6,3840]{2,0,1:T(2,128)(2,1)S(1)} %broadcast_select_fusion), kind=kOutput, calls=%fused_computation.2 | convolution fusion | flops 11059200 | bytes 3043584 | tf_op jit(solution)/shard_map/rsk,ski->rsi/dot_general | solution.py:47
  38.4 2.6 %copy.23 = bf16[96,2,3840]{2,1,0:T(2,128)(2,1)} copy(bf16[96,2,3840]{2,0,1:T(8,128)(2,1)S(1)} %fusion.1) | data formatting | bytes 2949120 | tf_op jit(solution)/shard_map/convert_element_type | solution.py:48
  (8 shorter events, 0.1 us)
Async XLA Ops:
  0.0 35.1 %copy-start = (f32[384,192]{0,1:T(8,128)S(1)}, f32[384,192]{0,1:T(8,128)}, u32[]{:S(2)}) copy-start(f32[384,192]{0,1:T(8,128)} %param.13) | copy-start | bytes 884740
  0.0 9.2 %copy-start.2 = (s32[1,24]{1,0:T(1,128)S(1)}, s32[1,24]{1,0:T(1,128)}, u32[]{:S(2)}) copy-start(s32[1,24]{1,0:T(1,128)} %param.12) | copy-start | bytes 292
  6.9 31.0 %copy-start.1 = (bf16[96,2,3840]{2,1,0:T(2,128)(2,1)S(1)}, bf16[96,2,3840]{2,1,0:T(2,128)(2,1)}, u32[]{:S(2)}) copy-start(bf16[96,2,3840]{2,1,0:T(2,128)(2,1)} %param.7) | copy-start | bytes 4423684
  9.5 7.1 %collective-permute-start = (f32[96,384]{1,0:T(8,128)S(1)}, f32[96,384]{1,0:T(8,128)S(1)}, u32[]{:S(2)}, u32[]{:S(2)}) collective-permute-start(f32[96,384]{1,0:T(8,128)S(1)} %fusion.11), channel_id=1, source_target_pairs={{0,2},{2,0},{4,6},{6,4},{8,10},{10,8},{12,14},{14,12},{16,18},{18,... | collective-permute-start | bytes 442376 | tf_op jit(solution)/shard_map/ppermute | solution.py:11
  16.6 5.4 %collective-permute-start.1 = (f32[96,384]{1,0:T(8,128)S(1)}, f32[96,384]{1,0:T(8,128)S(1)}, u32[]{:S(2)}, u32[]{:S(2)}) collective-permute-start(f32[96,384]{1,0:T(8,128)S(1)} %add.19), channel_id=1, source_target_pairs={{0,4},{2,6},{4,0},{6,2},{8,12},{10,14},{12,8},{14,10},{16,20},{18,... | collective-permute-start | bytes 442376 | tf_op jit(solution)/shard_map/ppermute | solution.py:11
  22.0 5.2 %collective-permute-start.2 = (f32[96,384]{1,0:T(8,128)S(1)}, f32[96,384]{1,0:T(8,128)S(1)}, u32[]{:S(2)}, u32[]{:S(2)}) collective-permute-start(f32[96,384]{1,0:T(8,128)S(1)} %add.20), channel_id=1, source_target_pairs={{0,8},{2,10},{4,12},{6,14},{8,0},{10,2},{12,4},{14,6},{16,24},{18,... | collective-permute-start | bytes 442376 | tf_op jit(solution)/shard_map/ppermute | solution.py:11
  27.2 7.8 %collective-permute-start.3 = (f32[96,384]{1,0:T(8,128)S(1)}, f32[96,384]{1,0:T(8,128)S(1)}, u32[]{:S(2)}, u32[]{:S(2)}) collective-permute-start(f32[96,384]{1,0:T(8,128)S(1)} %add.21), channel_id=1, source_target_pairs={{0,16},{2,18},{4,20},{6,22},{8,24},{10,26},{12,28},{14,30},{16,0},... | collective-permute-start | bytes 442376 | tf_op jit(solution)/shard_map/ppermute | solution.py:11
